TPU v7x, 512 devices: a whole 4x4x16 slice. The times are simulated.
512 devices in a mesh: ctx: 64 (over y, z), head: 8 (over x, core).
Axes of the slice: x: 4, y: 4, z: 16, core: 2. Of those that a mesh axis runs over, the one named last changes fastest.
Arguments:
- queries: bfloat16 [32768, 2048], P('ctx', 'head'), may hold values from -16 to 16
- keys: bfloat16 [32768, 2048], P('ctx', 'head'), may hold values from -16 to 16
- values: bfloat16 [32768, 2048], P('ctx', 'head'), may hold values from -12 to 12
- gain: bfloat16 [2048], P('head'), may hold values from 0.5 to 1.5
- cotangent: bfloat16 [32768, 2048], P('ctx', 'head'), may hold values from -6 to 6
Outputs:
- output: bfloat16 [32768, 2048], P('ctx', 'head')
- grad_queries: bfloat16 [32768, 2048], P('ctx', 'head')
- grad_keys: bfloat16 [32768, 2048], P('ctx', 'head')
- grad_values: bfloat16 [32768, 2048], P('ctx', 'head')
All inputs are finite; a program needn't handle non-finite values.
Results may differ from a plain program's by a relative error of at most 0.0065.
Values may be sent and summed in bfloat16 or wider, within the bound.
A program may use at most 64 MiB of HBM per device.

v0:
```python
import math

import jax
import jax.numpy as jnp
from jax import lax
from jax.sharding import PartitionSpec as P

HEAD_DIM = 128
WINDOW = 256


epsilon = 1e-06


def passed_along(value, axis, steps):
    count = lax.axis_size(axis)
    initial, last = (max(0, -steps), min(count, count - steps))
    return lax.ppermute(value, axis, [(source, source + steps) for source in range(initial, last)])


def prefix_2(part, axis, combine, identity, reverse):
    count = lax.axis_size(axis)
    place = lax.axis_index(axis)
    ahead = count - 1 - place if reverse else place
    gathered = lax.all_gather(part, axis)
    state = jnp.zeros_like(part) + jnp.asarray(identity, part.dtype)

    def one(step, state):
        source = count - 1 - step if reverse else step
        return combine(state, lax.dynamic_index_in_dim(gathered, source, 0, False))

    return lax.fori_loop(0, ahead, one, state)


def add_states(earlier, later):
    return earlier + later


def mixed(form, left, right):
    return jnp.einsum(form, left, right, preferred_element_type=jnp.float32)


def on_device(queries, keys, values, gain, cotangent):
    tok_rows, row_width = queries.shape
    heads_here = row_width // HEAD_DIM
    inv_root = 1.0 / math.sqrt(HEAD_DIM)
    features = row_width * lax.axis_size("head")
    block_index = lax.axis_index("ctx")
    offsets = jnp.arange(tok_rows, dtype=jnp.int32)
    positions = block_index * tok_rows + offsets
    coefs = 1.0 / jnp.sqrt(HEAD_DIM * (positions + 1).astype(jnp.float32))
    causal = (offsets[:, None] >= offsets[None, :])[None]
    ext_cols = jnp.arange(tok_rows + WINDOW, dtype=jnp.int32)
    window_mask = (
        (ext_cols[None, :] > offsets[:, None])
        & (ext_cols[None, :] <= offsets[:, None] + WINDOW)
        & (block_index * tok_rows - WINDOW + ext_cols[None, :] >= 0)
    )[None]
    query_heads = queries.reshape(tok_rows, heads_here, HEAD_DIM)
    key_heads = keys.reshape(tok_rows, heads_here, HEAD_DIM)
    value_heads = values.reshape(tok_rows, heads_here, HEAD_DIM)
    key_prev, value_prev = passed_along(
        (keys[tok_rows - WINDOW :], values[tok_rows - WINDOW :]), "ctx", 1
    )
    key_ext = jnp.concatenate([key_prev, keys], 0).reshape(tok_rows + WINDOW, heads_here, HEAD_DIM)
    value_ext = jnp.concatenate([value_prev, values], 0).reshape(
        tok_rows + WINDOW, heads_here, HEAD_DIM
    )
    local_state = mixed("tde,tdf->def", key_heads, value_heads)
    prefix = prefix_2(local_state, "ctx", add_states, jnp.zeros_like(local_state), False)
    prefix_b = prefix.astype(jnp.bfloat16)
    lin_weights = jnp.where(
        causal, mixed("tde,sde->dts", query_heads, key_heads) * coefs[None, :, None], 0.0
    ).astype(jnp.bfloat16)
    linear = coefs[:, None, None] * mixed("tde,def->tdf", query_heads, prefix_b)
    linear = linear + mixed("dts,sde->tde", lin_weights, value_heads)
    logits = mixed("tde,sde->dts", query_heads, key_ext) * inv_root
    row_peak = jnp.max(jnp.where(window_mask, logits, -1e30), -1)
    row_total = jnp.sum(jnp.where(window_mask, jnp.exp(logits - row_peak[..., None]), 0.0), -1)
    log_total = row_peak + jnp.log(row_total)
    probs = jnp.where(window_mask, jnp.exp(logits - log_total[..., None]), 0.0)
    probs_b = probs.astype(jnp.bfloat16)
    local_window = mixed("dts,sde->tde", probs_b, value_ext)
    hidden = (linear + local_window).reshape(tok_rows, row_width)
    gain_f = gain.astype(jnp.float32)
    scaled = gain_f[None, :] * cotangent.astype(jnp.float32)
    squares, crossed = lax.psum((jnp.sum(hidden * hidden, 1), jnp.sum(hidden * scaled, 1)), "head")
    recip = 1.0 / jnp.sqrt(squares / features + epsilon)
    output = (hidden * recip[:, None] * gain_f[None, :]).astype(jnp.bfloat16)
    grad_full = recip[:, None] * scaled - hidden * (recip**3 * crossed / features)[:, None]
    grad_b = grad_full.astype(jnp.bfloat16)
    grad_u = (grad_full * coefs[:, None]).astype(jnp.bfloat16)
    grad_heads = grad_b.reshape(tok_rows, heads_here, HEAD_DIM)
    gradu_heads = grad_u.reshape(tok_rows, heads_here, HEAD_DIM)
    local_suffix = mixed("tde,tdf->def", query_heads, gradu_heads)
    suffix = prefix_2(local_suffix, "ctx", add_states, jnp.zeros_like(local_suffix), True)
    suffix_b = suffix.astype(jnp.bfloat16)
    back_lin = jnp.where(causal, mixed("tde,sde->dts", gradu_heads, value_heads), 0.0).astype(
        jnp.bfloat16
    )
    d_query = mixed("tdf,def->tde", gradu_heads, prefix_b) + mixed(
        "dts,sde->tde", back_lin, key_heads
    )
    d_key = mixed("dts,tde->sde", back_lin, query_heads) + mixed(
        "sdf,def->sde", value_heads, suffix_b
    )
    d_value = mixed("dts,tde->sde", lin_weights, grad_heads) + mixed(
        "sde,def->sdf", key_heads, suffix_b
    )
    delta = jnp.sum(grad_heads.astype(jnp.float32) * local_window, -1).T
    d_probs = mixed("tde,sde->dts", grad_heads, value_ext)
    d_logits = (probs * (d_probs - delta[..., None]) * inv_root).astype(jnp.bfloat16)
    d_query = d_query + mixed("dts,sde->tde", d_logits, key_ext)
    d_key_ext = mixed("dts,tde->sde", d_logits, query_heads)
    d_value_ext = mixed("dts,tde->sde", probs_b, grad_heads)
    back_key, back_value = (
        passed_along(d_key_ext[:WINDOW].astype(jnp.bfloat16), "ctx", -1).astype(jnp.float32),
        passed_along(d_value_ext[:WINDOW].astype(jnp.bfloat16), "ctx", -1).astype(jnp.float32),
    )
    own_key = d_key_ext[WINDOW:]
    own_value = d_value_ext[WINDOW:]
    pad_rows = jnp.zeros((tok_rows - WINDOW, heads_here, HEAD_DIM), jnp.float32)
    d_key = d_key + own_key + jnp.concatenate([pad_rows, back_key], 0)
    d_value = d_value + own_value + jnp.concatenate([pad_rows, back_value], 0)
    grad_queries = d_query.reshape(tok_rows, row_width).astype(jnp.bfloat16)
    grad_keys = d_key.reshape(tok_rows, row_width).astype(jnp.bfloat16)
    grad_values = d_value.reshape(tok_rows, row_width).astype(jnp.bfloat16)
    return (output, grad_queries, grad_keys, grad_values)


def solution(mesh):
    return jax.shard_map(
        on_device,
        mesh=mesh,
        in_specs=(
            P("ctx", "head"),
            P("ctx", "head"),
            P("ctx", "head"),
            P("head"),
            P("ctx", "head"),
        ),
        out_specs=(P("ctx", "head"), P("ctx", "head"), P("ctx", "head"), P("ctx", "head")),
        check_vma=False,
    )
```

profile of v0, /device:TPU:1, one launch (start us, length us, event | category | flops | bytes accessed | tf_op | source)
XLA Modules:
  0.0 475.2 jit_solution(9685659801291127460)
XLA Ops:
  8.3 1.9 fusion.26
  11.3 4.4 collective-permute-start
  15.7 3.5 collective-permute-start.1
  21.1 2.5 select_convert_fusion.1
  27.1 1.9 fusion
  29.0 1.7 fusion.3
  30.8 1.8 convolution_bitcast_fusion.3
  32.6 133.5 %all-gather.5.cloned.1.call-done = f32[128,128,128]{2,1,0:T(8,128)} async-done(((f32[2,128,128]{2,1,0:T(8,128)}), f32[128,128,128]{2,1,0:T(8,128)}) %all-gather.5.cloned.1.call-update) | async-done | bytes 8388624 | tf_op jit(solution)/shard_map/all_gather | solution.py:25
  166.4 2.8 multiply_reduce_fusion.2
  169.2 2.0 copy.96
  172.5 20.8 %all-reduce.2 = (f32[512]{0:T(512)}, f32[512]{0:T(512)}) all-reduce(f32[512]{0:T(512)S(1)} %get-tuple-element.130, f32[512]{0:T(512)S(1)} %multiply_reduce_fusion.1), channel_id=1, replica_groups=mesh['ctx'=64,'head'=8] {'head'}, use_global_device_ids=true, to_apply=%region_5.6 | all-reduce | flops 1024 | bytes 8192 | tf_op jit(solution)/shard_map/psum | solution.py:87
  194.0 2.3 fusion.19
  196.3 1.8 copy.132
  198.1 1.8 convolution_bitcast_fusion.9
  199.9 1.6 copy.111
  201.6 1.8 copy.103
  205.8 1.7 select_convert_fusion
  212.1 1.8 copy.118
  213.9 2.0 convolution_bitcast_fusion.1
  217.6 2.0 convolution_bitcast_fusion
  223.8 176.4 %all-gather.7.cloned.1.call-done = f32[128,128,128]{2,1,0:T(8,128)} async-done(((f32[2,128,128]{2,1,0:T(8,128)}), f32[128,128,128]{2,1,0:T(8,128)}) %all-gather.7.cloned.1.call-update) | async-done | bytes 8388624 | tf_op jit(solution)/shard_map/all_gather | solution.py:25
  400.2 60.6 %while.23 = (s32[]{:T(128)}, f32[2,128,128]{2,1,0:T(8,128)S(1)}, s32[]{:T(128)}, f32[64,2,128,128]{3,2,1,0:T(8,128)}, s32[]{:T(128)}, /*index=5*/s32[]{:T(128)}, s32[]{:T(128)}, s32[]{:T(128)}) while((s32[]{:T(128)}, f32[2,128,128]{2,1,0:T(8,128)S(1)}, s32[]{:T(128)}, f32[64,2,128,128]{3,2,1,0:T(8,128)}, s32[]{:T(128)}, ...), condition=%wide.region_10.11_spmd, body=%wide.region_9.10_spmd.sunk | while | flops 32774 | bytes 393359 | solution.py:32
  462.0 2.2 add_convert_fusion
  464.2 1.8 copy.120
  (144 shorter events, 85.2 us)
Async XLA Ops:
  7.2 18.2 %copy-start.1 = (bf16[512,256]{1,0:T(8,128)(2,1)S(1)}, bf16[512,256]{1,0:T(8,128)(2,1)}, u32[]{:S(2)}) copy-start(bf16[512,256]{1,0:T(8,128)(2,1)} %param.11) | copy-start | bytes 786436
  7.2 17.6 %copy-start.19 = (bf16[256]{0:T(256)(128)(2,1)S(1)}, bf16[256]{0:T(256)(128)(2,1)}, u32[]{:S(2)}) copy-start(bf16[256]{0:T(256)(128)(2,1)} %param.12) | copy-start | bytes 1540
  7.2 158.9 %all-gather.5.cloned.1.call-start = ((), (), s32[]{:S(2)}) async-start(), calls=%async_computation | async-start | bytes 8519680 | tf_op jit(solution)/shard_map/all_gather | solution.py:25
  8.3 18.0 %copy-start.3 = (bf16[512,256]{0,1:T(8,128)(2,1)}, bf16[512,256]{0,1:T(8,128)(2,1)S(1)}, u32[]{:S(2)}) copy-start(bf16[512,256]{0,1:T(8,128)(2,1)S(1)} %copy.91) | copy-start | bytes 786436
  10.3 389.8 %all-gather.7.cloned.1.call-start = ((), (), s32[]{:S(2)}) async-start(), calls=%async_computation.1 | async-start | bytes 8519680 | tf_op jit(solution)/shard_map/all_gather | solution.py:25
  11.3 14.1 %collective-permute-start = (bf16[256,256]{1,0:T(8,128)(2,1)S(1)}, bf16[256,256]{1,0:T(8,128)(2,1)S(1)}, u32[]{:S(2)}, u32[]{:S(2)}) collective-permute-start(bf16[256,256]{1,0:T(8,128)(2,1)S(1)} %slice.20), channel_id=1, source_target_pairs={{0,8},{8,16},{16,24},{24,32},{32,40},{40,48},{48,56},{56,64},{64,7... | collective-permute-start | bytes 393224 | tf_op jit(solution)/shard_map/ppermute | solution.py:18
  15.7 10.6 %collective-permute-start.1 = (bf16[256,256]{0,1:T(8,128)(2,1)S(1)}, bf16[256,256]{0,1:T(8,128)(2,1)S(1)}, u32[]{:S(2)}, u32[]{:S(2)}) collective-permute-start(bf16[256,256]{0,1:T(8,128)(2,1)S(1)} %slice.26), channel_id=1, source_target_pairs={{0,8},{8,16},{16,24},{24,32},{32,40},{40,48},{48,56},{56,64},{64,7... | collective-permute-start | bytes 393224 | tf_op jit(solution)/shard_map/ppermute | solution.py:18
  27.1 3.7 copy-start.8
  27.1 3.7 copy-start.16
  203.4 4.1 copy-start.4
  203.4 5.1 %copy-start.9 = (pred[512,768]{0,1:T(8,128)(4,1)S(1)}, pred[512,768]{0,1:T(8,128)(4,1)}, u32[]{:S(2)}) copy-start(pred[512,768]{0,1:T(8,128)(4,1)} %fusion.8) | copy-start | bytes 1179652
  203.4 5.1 %copy-start.14 = (bf16[512,256]{0,1:T(8,128)(2,1)S(1)}, bf16[512,256]{0,1:T(8,128)(2,1)}, u32[]{:S(2)}) copy-start(bf16[512,256]{0,1:T(8,128)(2,1)} %copy.103) | copy-start | bytes 786436
  203.4 5.1 %copy-start.17 = (bf16[768,256]{0,1:T(8,128)(2,1)S(1)}, bf16[768,256]{0,1:T(8,128)(2,1)}, u32[]{:S(2)}) copy-start(bf16[768,256]{0,1:T(8,128)(2,1)} %copy.90) | copy-start | bytes 1179652
  207.5 1.0 copy-start.6
  208.5 2.5 copy-start.11
  209.8 1.2 copy-start
  215.9 1.0 copy-start.12
  219.6 0.9 copy-start.15
  220.5 241.5 %copy-start.5 = (bf16[2,512,512]{2,1,0:T(8,128)(2,1)S(1)}, bf16[2,512,512]{2,1,0:T(8,128)(2,1)}, u32[]{:S(2)}) copy-start(bf16[2,512,512]{2,1,0:T(8,128)(2,1)} %select_convert_fusion.1) | copy-start | bytes 3145732
  221.2 240.8 %collective-permute-start.3 = (bf16[256,2,128]{0,2,1:T(8,128)(2,1)}, bf16[256,2,128]{0,2,1:T(8,128)(2,1)}, u32[]{:S(2)}, u32[]{:S(2)}) collective-permute-start(bf16[256,2,128]{0,2,1:T(8,128)(2,1)} %slice.35), channel_id=1, source_target_pairs={{8,0},{16,8},{24,16},{32,24},{40,32},{48,40},{56,48},{64,56},{72,6... | collective-permute-start | bytes 393224 | tf_op jit(solution)/shard_map/ppermute | solution.py:18
  222.4 243.8 %collective-permute-start.2 = (bf16[256,2,128]{0,2,1:T(8,128)(2,1)}, bf16[256,2,128]{0,2,1:T(8,128)(2,1)}, u32[]{:S(2)}, u32[]{:S(2)}) collective-permute-start(bf16[256,2,128]{0,2,1:T(8,128)(2,1)} %slice.36), channel_id=1, source_target_pairs={{8,0},{16,8},{24,16},{32,24},{40,32},{48,40},{56,48},{64,56},{72,6... | collective-permute-start | bytes 393224 | tf_op jit(solution)/shard_map/ppermute | solution.py:18
  400.1 65.9 %copy-start.2 = (bf16[512,256]{1,0:T(8,128)(2,1)S(1)}, bf16[512,256]{1,0:T(8,128)(2,1)}, u32[]{:S(2)}) copy-start(bf16[512,256]{1,0:T(8,128)(2,1)} %param.11) | copy-start | bytes 786436
  400.2 66.1 %copy-start.7 = (bf16[2,512,512]{2,1,0:T(8,128)(2,1)S(1)}, bf16[2,512,512]{2,1,0:T(8,128)(2,1)}, u32[]{:S(2)}) copy-start(bf16[2,512,512]{2,1,0:T(8,128)(2,1)} %copy-done.6) | copy-start | bytes 3145732
  400.2 66.1 %copy-start.13 = (f32[768,2,128]{0,2,1:T(8,128)S(1)}, f32[768,2,128]{0,2,1:T(8,128)}, u32[]{:S(2)}) copy-start(f32[768,2,128]{0,2,1:T(8,128)} %copy-done.12) | copy-start | bytes 2359300
  (2 other events, 1.5 us)
Sparse Core Ops, SparseCore 0:
  11.5 154.5 all-gather.4
  201.7 198.4 all-gather.6
where the time goes:
time: 484 us; the launch traced here: 475 us
  waiting for transfers between devices  310 us (64%)
  other arithmetic  68.2 us (14%)
  matrix products  27.6 us (6%)
  local copies, waits for them, and re-layouts  22.1 us (5%)
  blocking collectives  20.8 us (4%)
  between operations  14.4 us (3%)
  starting transfers between devices  10.6 us (2%)
    all_gather x2, waiting for transfers between devices, prefix_2(): gathered = lax.all_gather(part, axis)  310 us
    add x63, other arithmetic, add_states(): return earlier + later  59.2 us
    dot_general x18, matrix products, mixed(): return jnp.einsum(form, left, right, preferred_element_type=jnp.float32)  27.6 us
    psum x1, blocking collectives, on_device(): lax.psum((jnp.sum(hidden * hidden, 1), jnp.sum(hidden * scaled, 1)), 'head')  20.8 us
    unnamed x44, local copies, waits for them, and re-layouts  10.5 us
    ppermute x4, starting transfers between devices, passed_along(): lax.ppermute(value, axis, [(source, source + steps) for source in range(i...  10.5 us
  transfers between devices with their start and end apart: 6, of which 2 were waited for; matrix products, arithmetic and copies ran while one was open for 20% of the time, Pallas kernels for 0%

commit v1 on v0

v1 whole, which is shorter than its diff:
```python
import functools
import math

import jax
import jax.numpy as jnp
from jax import lax
from jax.experimental import pallas as pl
from jax.experimental.pallas import tpu as pltpu
from jax.sharding import PartitionSpec as P

HEAD_DIM = 128
WINDOW = 256
HALF = 256
EPS = 1e-06
MESH = pl.DeviceIdType.MESH
F32 = jnp.float32
BF16 = jnp.bfloat16


def dot(left, right, left_dim, right_dim):
    return lax.dot_general(
        left, right, (((left_dim,), (right_dim,)), ((), ())), preferred_element_type=F32
    )


def nn(left, right):
    return dot(left, right, 1, 0)


def nt(left, right):
    return dot(left, right, 1, 1)


def tn(left, right):
    return dot(left, right, 0, 0)


def kernel(
    n_ctx, n_z, n_head,
    q_hbm, k_hbm, v_hbm, gain_hbm, cot_hbm,
    out_hbm, dq_hbm, dk_hbm, dv_hbm,
    q, k, v, gain, cot,
    k_halo, v_halo, dk_give, dv_give, dk_take, dv_take,
    scat_f, got_f, back_f, pre, scat_b, got_b, back_b, post, flat,
    stat_mine, stat_all,
    probs, w_own, w_prev, local, scaled_t, grad_t, gradu_t,
    dk_acc, dv_acc, out, dq, dk, dv,
    in_sem, out_sem, scan_send, scan_recv, halo_send, halo_recv, stat_send, stat_recv,
):
    me = lax.axis_index("ctx")
    mine = lax.axis_index("head")
    n_y = n_ctx // n_z
    my_y = me // n_z
    my_z = lax.rem(me, n_z)
    following = lax.rem(me + 1, n_ctx)
    before = lax.rem(me + n_ctx - 1, n_ctx)
    rows = 256 // n_ctx
    tokens = 2 * HALF
    features = 256 * n_head
    scale = 1.0 / math.sqrt(HEAD_DIM)

    barrier = pltpu.get_barrier_semaphore()

    def greet(step, carry):
        pl.semaphore_signal(
            barrier, inc=1, device_id={"ctx": lax.rem(me + step, n_ctx), "head": mine},
            device_id_type=MESH,
        )
        return carry

    lax.fori_loop(1, n_ctx, greet, 0)
    for step in range(1, n_head):
        pl.semaphore_signal(
            barrier, inc=1, device_id={"ctx": me, "head": lax.rem(mine + step, n_head)},
            device_id_type=MESH,
        )

    loads = [
        pltpu.make_async_copy(src, dst, in_sem.at[i])
        for i, (src, dst) in enumerate(
            ((k_hbm, k), (v_hbm, v), (q_hbm, q), (cot_hbm, cot), (gain_hbm, gain))
        )
    ]
    for load in loads:
        load.start()

    y_order = sorted(range(n_y), key=lambda d: -min(d, n_y - d))

    def exchange(src, dst, phase):
        def send(away_y, away_z):
            target = lax.rem(my_y + away_y, n_y) * n_z + lax.rem(my_z + away_z, n_z)
            pltpu.make_async_remote_copy(
                src.at[target], dst.at[me], scan_send.at[phase], scan_recv.at[phase],
                device_id={"ctx": target, "head": mine}, device_id_type=MESH,
            ).start()

        def step(i, carry):
            away_z = n_z // 2 + ((i + 1) // 2) * (1 - 2 * lax.rem(i, 2))
            for away_y in y_order:
                send(away_y, away_z)
            return carry

        lax.fori_loop(0, n_z - 1, step, 0)
        for away_y in y_order:
            if away_y:
                send(away_y, 0)
        dst[pl.ds(me, 1)] = src[pl.ds(me, 1)]

    def arrived(dst, phase):
        part = dst.at[pl.ds(0, n_ctx - 1)]
        pltpu.make_async_copy(part, part, scan_recv.at[phase]).wait()

    def left(src, phase):
        part = src.at[pl.ds(0, n_ctx - 1)]
        pltpu.make_async_copy(part, part, scan_send.at[phase]).wait()

    def scatter(state, head, dst):
        for i in range(HEAD_DIM // rows):
            dst[head * (HEAD_DIM // rows) + i] = state[i * rows : (i + 1) * rows].astype(BF16)

    def running(src, dst, order):
        total = jnp.zeros((rows, HEAD_DIM), F32)
        for i in order:
            dst[i] = total.astype(BF16)
            total = total + src[i].astype(F32)

    def collect(src, dst):
        for i in range(n_ctx):
            dst[i * rows : (i + 1) * rows, :] = src[i].astype(F32)

    cols = [slice(h * HEAD_DIM, (h + 1) * HEAD_DIM) for h in range(2)]
    half = [slice(b * HALF, (b + 1) * HALF) for b in range(2)]

    loads[0].wait()
    loads[1].wait()
    for h in range(2):
        scatter(tn(v[:, cols[h]], k[:, cols[h]]), h, scat_f)
    pl.semaphore_wait(barrier, n_ctx - 1 + n_head - 1)
    exchange(scat_f, got_f, 0)
    halo_out = [
        pltpu.make_async_remote_copy(
            src.at[pl.ds(HALF, HALF)], dst, halo_send.at[i], halo_recv.at[i],
            device_id={"ctx": following, "head": mine}, device_id_type=MESH,
        )
        for i, (src, dst) in enumerate(((k, k_halo), (v, v_halo)))
    ]
    for copy in halo_out:
        copy.start()

    for load in loads[2:]:
        load.wait()
    position = me * tokens + lax.broadcasted_iota(jnp.int32, (1, tokens), 1)
    coef = 1.0 / jnp.sqrt(HEAD_DIM * (position + 1).astype(F32))
    lower = lax.broadcasted_iota(jnp.int32, (HALF, HALF), 0) > lax.broadcasted_iota(
        jnp.int32, (HALF, HALF), 1
    )
    no_halo = jnp.where(me == 0, -1e30, 0.0).astype(F32)
    scaled_t[...] = (gain[...].astype(F32) * cot[...].astype(F32)).T

    def near(b, h, own, halo):
        prev_part = halo[:, cols[h]] if b == 0 else own[half[0], cols[h]]
        return prev_part, own[half[b], cols[h]]

    def forward(b, h):
        query = q[half[b], cols[h]]
        key_prev, key_own = near(b, h, k, k_halo)
        value_prev, value_own = near(b, h, v, v_halo)
        prev = nt(key_prev, query)
        own = nt(key_own, query)
        c = coef[:, half[b]]
        logits = jnp.where(lower, prev + no_halo if b == 0 else prev, own)
        peak = jnp.max(logits, 0, keepdims=True)
        weight = jnp.exp((logits - peak) * scale)
        weight = weight * (1.0 / jnp.sum(weight, 0, keepdims=True))
        probs[h, b] = weight
        mix_own = jnp.where(lower, 0.0, weight + c * own).astype(BF16)
        mix_prev = jnp.where(lower, weight, 0.0)
        if b == 1:
            mix_prev = mix_prev + c * prev
        mix_prev = mix_prev.astype(BF16)
        w_own[h, b] = mix_own
        w_prev[h, b] = mix_prev
        local[cols[h], half[b]] = tn(value_own, mix_own) + tn(value_prev, mix_prev)

    for h in range(2):
        forward(1, h)
    for copy in halo_out:
        copy.wait()
    for h in range(2):
        forward(0, h)

    arrived(got_f, 0)
    running(got_f, back_f, range(n_ctx))
    exchange(back_f, pre, 1)
    arrived(pre, 1)
    collect(pre, flat)
    prefix = flat[...].astype(BF16)

    hidden = []
    for h in range(2):
        hidden.append(local[cols[h], :] + coef * nt(prefix[cols[h], :], q[:, cols[h]]))
    squares = sum(jnp.sum(x * x, 0, keepdims=True) for x in hidden)
    crossed = sum(
        jnp.sum(x * scaled_t[cols[h], :], 0, keepdims=True) for h, x in enumerate(hidden)
    )
    stat_mine[0:1, :] = squares
    stat_mine[1:2, :] = crossed
    shares = [
        pltpu.make_async_remote_copy(
            stat_mine, stat_all.at[mine], stat_send, stat_recv,
            device_id={"ctx": me, "head": lax.rem(mine + step, n_head)}, device_id_type=MESH,
        )
        for step in range(n_head - 1, 0, -1)
    ]
    for copy in shares:
        copy.start()
    stat_all[pl.ds(mine, 1)] = stat_mine[...][None]
    for h in range(2):
        local[cols[h], :] = hidden[h]
    others = stat_all.at[pl.ds(0, n_head - 1)]
    pltpu.make_async_copy(others, others, stat_recv).wait()
    sums = stat_all[0]
    for i in range(1, n_head):
        sums = sums + stat_all[i]
    recip = 1.0 / jnp.sqrt(sums[0:1] / features + EPS)
    pull = recip * recip * recip * sums[1:2] / features

    for h in range(2):
        full = recip * scaled_t[cols[h], :] - local[cols[h], :] * pull
        grad_t[cols[h], :] = full.astype(BF16)
        grad_u = (full * coef).astype(BF16)
        gradu_t[cols[h], :] = grad_u
        scatter(nn(grad_u, q[:, cols[h]]), h, scat_b)
    exchange(scat_b, got_b, 2)

    dk_acc[...] = jnp.zeros_like(dk_acc)
    dv_acc[...] = jnp.zeros_like(dv_acc)

    def backward(b, h):
        query = q[half[b], cols[h]]
        key_prev, key_own = near(b, h, k, k_halo)
        value_prev, value_own = near(b, h, v, v_halo)
        grad = grad_t[cols[h], half[b]]
        c = coef[:, half[b]]
        prev = nn(value_prev, grad)
        own = nn(value_own, grad)
        weight = probs[h, b]
        pulled = jnp.where(lower, prev, own)
        delta = jnp.sum(weight * pulled, 0, keepdims=True)
        d_logits = weight * (pulled - delta) * scale
        d_own = jnp.where(lower, 0.0, d_logits + c * own).astype(BF16)
        d_prev = jnp.where(lower, d_logits, 0.0)
        if b == 1:
            d_prev = d_prev + c * prev
        d_prev = d_prev.astype(BF16)
        far = tn(gradu_t[cols[h], half[b]], prefix[cols[h], :])
        dq[half[b], cols[h]] = (far + tn(d_own, key_own) + tn(d_prev, key_prev)).astype(BF16)
        dk_acc[half[b], cols[h]] += nn(d_own, query)
        dv_acc[half[b], cols[h]] += nt(w_own[h, b], grad)
        if b == 0:
            dk_give[:, cols[h]] = nn(d_prev, query).astype(BF16)
            dv_give[:, cols[h]] = nt(w_prev[h, b], grad).astype(BF16)
        else:
            dk_acc[half[0], cols[h]] += nn(d_prev, query)
            dv_acc[half[0], cols[h]] += nt(w_prev[h, b], grad)

    for h in range(2):
        backward(0, h)
    halo_back = [
        pltpu.make_async_remote_copy(
            src, dst, halo_send.at[2 + i], halo_recv.at[2 + i],
            device_id={"ctx": before, "head": mine}, device_id_type=MESH,
        )
        for i, (src, dst) in enumerate(((dk_give, dk_take), (dv_give, dv_take)))
    ]
    for copy in halo_back:
        copy.start()
    for h in range(2):
        backward(1, h)
    store_dq = pltpu.make_async_copy(dq, dq_hbm, out_sem.at[0])
    store_dq.start()

    arrived(got_b, 2)
    running(got_b, back_b, range(n_ctx - 1, -1, -1))
    exchange(back_b, post, 3)

    out[...] = ((local[...] * recip).T * gain[...].astype(F32)).astype(BF16)
    store_out = pltpu.make_async_copy(out, out_hbm, out_sem.at[1])
    store_out.start()
    for copy in halo_back:
        copy.wait()
    dk_acc[half[1], :] += dk_take[...].astype(F32)
    dv_acc[half[1], :] += dv_take[...].astype(F32)

    arrived(post, 3)
    collect(post, flat)
    suffix = flat[...].astype(BF16)
    for h in range(2):
        dk[:, cols[h]] = (dk_acc[:, cols[h]] + nn(v[:, cols[h]], suffix[cols[h], :])).astype(BF16)
    store_dk = pltpu.make_async_copy(dk, dk_hbm, out_sem.at[2])
    store_dk.start()
    for h in range(2):
        dv[:, cols[h]] = (dv_acc[:, cols[h]] + nt(k[:, cols[h]], suffix[cols[h], :])).astype(BF16)
    store_dv = pltpu.make_async_copy(dv, dv_hbm, out_sem.at[3])
    store_dv.start()

    for phase, src in enumerate((scat_f, back_f, scat_b, back_b)):
        left(src, phase)
    sent = stat_all.at[pl.ds(0, n_head - 1)]
    pltpu.make_async_copy(sent, sent, stat_send).wait()
    for copy in (store_dq, store_out, store_dk, store_dv):
        copy.wait()


def on_device(n_ctx, n_z, n_head, queries, keys, values, gain, cotangent):
    tokens, width = queries.shape
    pieces = (n_ctx, 256 // n_ctx, HEAD_DIM)
    block = jax.ShapeDtypeStruct((tokens, width), BF16)
    wide = pltpu.VMEM((tokens, width), BF16)
    halo = pltpu.VMEM((HALF, width), BF16)
    piece = pltpu.VMEM(pieces, BF16)
    square = (2, 2, HALF, HALF)
    turned = (width, tokens)
    return pl.pallas_call(
        functools.partial(kernel, n_ctx, n_z, n_head),
        out_shape=[block] * 4,
        in_specs=[pl.BlockSpec(memory_space=pl.ANY)] * 5,
        out_specs=[pl.BlockSpec(memory_space=pl.ANY)] * 4,
        scratch_shapes=[
            wide, wide, wide, pltpu.VMEM((1, width), BF16), wide,
            halo, halo, halo, halo, halo, halo,
            piece, piece, piece, piece, piece, piece, piece, piece,
            pltpu.VMEM((256, HEAD_DIM), F32),
            pltpu.VMEM((2, tokens), F32), pltpu.VMEM((n_head, 2, tokens), F32),
            pltpu.VMEM(square, F32), pltpu.VMEM(square, BF16), pltpu.VMEM(square, BF16),
            pltpu.VMEM(turned, F32), pltpu.VMEM(turned, F32),
            pltpu.VMEM(turned, BF16), pltpu.VMEM(turned, BF16),
            pltpu.VMEM((tokens, width), F32), pltpu.VMEM((tokens, width), F32),
            wide, wide, wide, wide,
            pltpu.SemaphoreType.DMA((5,)), pltpu.SemaphoreType.DMA((4,)),
            pltpu.SemaphoreType.DMA((4,)), pltpu.SemaphoreType.DMA((4,)),
            pltpu.SemaphoreType.DMA((4,)), pltpu.SemaphoreType.DMA((4,)),
            pltpu.SemaphoreType.DMA, pltpu.SemaphoreType.DMA,
        ],
        compiler_params=pltpu.CompilerParams(
            collective_id=0, has_side_effects=True, vmem_limit_bytes=48 << 20
        ),
    )(queries, keys, values, gain.reshape(1, width), cotangent)


def solution(mesh):
    n_ctx, n_head = mesh.shape["ctx"], mesh.shape["head"]
    n_z = 16 if n_ctx % 16 == 0 else n_ctx // 2
    return jax.shard_map(
        functools.partial(on_device, n_ctx, n_z, n_head),
        mesh=mesh,
        in_specs=(
            P("ctx", "head"), P("ctx", "head"), P("ctx", "head"), P("head"), P("ctx", "head"),
        ),
        out_specs=(P("ctx", "head"),) * 4,
        check_vma=False,
    )
```

time: 484 us -> 67.4 us (0.14); the launches traced: 475 us -> 67.1 us
  waiting for transfers between devices: 310 us -> 0 us
  other arithmetic: 68.2 us -> 0 us
  Pallas kernels: 0 us -> 59.2 us
  matrix products: 27.6 us -> 0 us
  blocking collectives: 20.8 us -> 0 us
  local copies, waits for them, and re-layouts: 22.1 us -> 7.27 us
  between operations: 14.4 us -> 0.64 us
  starting transfers between devices: 10.6 us -> 0 us
    all_gather x2 -> x0, waiting for transfers between devices: 310 us -> none  [prefix_2(): gathered = lax.all_gather(part, axis)]
    pallas_call x0 -> x1, Pallas kernels: none -> 59.2 us  [on_device(): pl.pallas_call(functools.partial(kernel, n_ctx, n_z, n_head), out_shape=[...]
    add x65 -> x0, other arithmetic: 59.2 us -> none  [the longest x63 59.2 us: add_states(): return earlier + later]
    dot_general x18 -> x0, matrix products: 27.6 us -> none  [mixed(): return jnp.einsum(form, left, right, preferred_element_type=jnp.float32)]
    psum x1 -> x0, blocking collectives: 20.8 us -> none  [on_device(): lax.psum((jnp.sum(hidden * hidden, 1), jnp.sum(hidden * scaled, 1)), 'head')]
    ppermute x4 -> x0, starting transfers between devices: 10.5 us -> none  [passed_along(): lax.ppermute(value, axis, [(source, source + steps) for source in range(i...]
    unnamed x44 -> x12, local copies, waits for them, and re-layouts: 10.5 us -> 6.61 us
  transfers between devices with their start and end apart: 6 -> 0, of which waited for: 2 -> 0; matrix products, arithmetic and copies ran while one was open for 20% -> 0% of each run, Pallas kernels for 0% -> 0%
where the time goes in v1:
time: 67.4 us; the launch traced here: 67.1 us
  Pallas kernels  59.2 us (88%)
  local copies, waits for them, and re-layouts  7.27 us (11%)
    pallas_call x1, Pallas kernels, on_device(): pl.pallas_call(functools.partial(kernel, n_ctx, n_z, n_head), out_shape=[...  59.2 us
    unnamed x12, local copies, waits for them, and re-layouts  6.61 us

profile of v1, /device:TPU:1, one launch (start us, length us, event | category | flops | bytes accessed | tf_op | source)
XLA Modules:
  0.0 67.1 jit_solution(1969638702929080770)
XLA Ops:
  0.6 0.7 reshape.11.gain_hbm
  1.3 0.0 copy-start
  1.3 0.9 %copy-done = bf16[512,256]{1,0:T(8,128)(2,1)S(1)} copy-done((bf16[512,256]{1,0:T(8,128)(2,1)S(1)}, bf16[512,256]{1,0:T(8,128)(2,1)}, u32[]{:S(2)}) %copy-start) | copy-done | bytes 262168
  2.2 0.0 copy-start.1
  2.2 0.9 %copy-done.1 = bf16[512,256]{1,0:T(8,128)(2,1)S(1)} copy-done((bf16[512,256]{1,0:T(8,128)(2,1)S(1)}, bf16[512,256]{1,0:T(8,128)(2,1)}, u32[]{:S(2)}) %copy-start.1) | copy-done | bytes 262168
  3.2 0.0 copy-start.2
  3.2 0.9 %copy-done.2 = bf16[512,256]{1,0:T(8,128)(2,1)S(1)} copy-done((bf16[512,256]{1,0:T(8,128)(2,1)S(1)}, bf16[512,256]{1,0:T(8,128)(2,1)}, u32[]{:S(2)}) %copy-start.2) | copy-done | bytes 262168
  4.1 0.0 copy-start.3
  4.1 0.9 %copy-done.3 = bf16[512,256]{1,0:T(8,128)(2,1)S(1)} copy-done((bf16[512,256]{1,0:T(8,128)(2,1)S(1)}, bf16[512,256]{1,0:T(8,128)(2,1)}, u32[]{:S(2)}) %copy-start.3) | copy-done | bytes 262168
  5.1 59.2 %shard_map.84 = (bf16[512,256]{1,0:T(8,128)(2,1)S(1)}, bf16[512,256]{1,0:T(8,128)(2,1)S(1)}, bf16[512,256]{1,0:T(8,128)(2,1)S(1)}, bf16[512,256]{1,0:T(8,128)(2,1)S(1)}) custom-call(bf16[512,256]{1,0:T(8,128)(2,1)S(1)} %copy-done, bf16[512,256]{1,0:T(8,128)(2,1)S(1)} %copy-done.1, bf16[512,256]{1,0:T(8,128)(2,1)S(1)} %copy-done.2, ...), custom_call_target="tpu_custom_call" | custom-call | tf_op jit(solution)/shard_map/pallas_call | solution.py:324
  64.3 0.7 %copy.13 = bf16[512,256]{1,0:T(8,128)(2,1)} copy(bf16[512,256]{1,0:T(8,128)(2,1)S(1)} %get-tuple-element.8) | data formatting | bytes 524288
  65.0 0.7 %copy.14 = bf16[512,256]{1,0:T(8,128)(2,1)} copy(bf16[512,256]{1,0:T(8,128)(2,1)S(1)} %get-tuple-element.9) | data formatting | bytes 524288
  65.7 0.7 %copy.15 = bf16[512,256]{1,0:T(8,128)(2,1)} copy(bf16[512,256]{1,0:T(8,128)(2,1)S(1)} %get-tuple-element.10) | data formatting | bytes 524288
  66.4 0.7 %copy.16 = bf16[512,256]{1,0:T(8,128)(2,1)} copy(bf16[512,256]{1,0:T(8,128)(2,1)S(1)} %get-tuple-element.11) | data formatting | bytes 524288
Async XLA Ops:
  1.3 0.9 %copy-start = (bf16[512,256]{1,0:T(8,128)(2,1)S(1)}, bf16[512,256]{1,0:T(8,128)(2,1)}, u32[]{:S(2)}) copy-start(bf16[512,256]{1,0:T(8,128)(2,1)} %q_hbm.1) | copy-start | bytes 786436
  2.2 0.9 %copy-start.1 = (bf16[512,256]{1,0:T(8,128)(2,1)S(1)}, bf16[512,256]{1,0:T(8,128)(2,1)}, u32[]{:S(2)}) copy-start(bf16[512,256]{1,0:T(8,128)(2,1)} %k_hbm.1) | copy-start | bytes 786436
  3.2 0.9 %copy-start.2 = (bf16[512,256]{1,0:T(8,128)(2,1)S(1)}, bf16[512,256]{1,0:T(8,128)(2,1)}, u32[]{:S(2)}) copy-start(bf16[512,256]{1,0:T(8,128)(2,1)} %v_hbm.1) | copy-start | bytes 786436
  4.1 0.9 %copy-start.3 = (bf16[512,256]{1,0:T(8,128)(2,1)S(1)}, bf16[512,256]{1,0:T(8,128)(2,1)}, u32[]{:S(2)}) copy-start(bf16[512,256]{1,0:T(8,128)(2,1)} %cot_hbm.1) | copy-start | bytes 786436

commit v2 on v1

--- a/solution.py
+++ b/solution.py
@@ -38,14 +38,13 @@
 def kernel(
     n_ctx, n_z, n_head,
     q_hbm, k_hbm, v_hbm, gain_hbm, cot_hbm,
-    out_hbm, dq_hbm, dk_hbm, dv_hbm,
-    q, k, v, gain, cot,
+    out, dq, dk_acc, dv_acc, suffix, k, v,
+    q, gain, cot,
     k_halo, v_halo, dk_give, dv_give, dk_take, dv_take,
     scat_f, got_f, back_f, pre, scat_b, got_b, back_b, post, flat,
     stat_mine, stat_all,
     probs, w_own, w_prev, local, scaled_t, grad_t, gradu_t,
-    dk_acc, dv_acc, out, dq, dk, dv,
-    in_sem, out_sem, scan_send, scan_recv, halo_send, halo_recv, stat_send, stat_recv,
+    in_sem, scan_send, scan_recv, halo_send, halo_recv, stat_send, stat_recv,
 ):
     me = lax.axis_index("ctx")
     mine = lax.axis_index("head")
@@ -61,19 +60,31 @@
 
     barrier = pltpu.get_barrier_semaphore()
 
-    def greet(step, carry):
+    y_order = sorted(range(n_y), key=lambda d: -min(d, n_y - d))
+
+    def farthest_first(visit):
+        def at(away_y, away_z):
+            visit(lax.rem(my_y + away_y, n_y) * n_z + lax.rem(my_z + away_z, n_z))
+
+        def step(i, carry):
+            away_z = n_z // 2 + ((i + 1) // 2) * (1 - 2 * lax.rem(i, 2))
+            for away_y in y_order:
+                at(away_y, away_z)
+            return carry
+
+        lax.fori_loop(0, n_z - 1, step, 0)
+        for away_y in y_order:
+            if away_y:
+                at(away_y, 0)
+
+    def greet(target, head):
         pl.semaphore_signal(
-            barrier, inc=1, device_id={"ctx": lax.rem(me + step, n_ctx), "head": mine},
-            device_id_type=MESH,
-        )
-        return carry
-
-    lax.fori_loop(1, n_ctx, greet, 0)
+            barrier, inc=1, device_id={"ctx": target, "head": head}, device_id_type=MESH
+        )
+
+    farthest_first(lambda target: greet(target, mine))
     for step in range(1, n_head):
-        pl.semaphore_signal(
-            barrier, inc=1, device_id={"ctx": me, "head": lax.rem(mine + step, n_head)},
-            device_id_type=MESH,
-        )
+        greet(me, lax.rem(mine + step, n_head))
 
     loads = [
         pltpu.make_async_copy(src, dst, in_sem.at[i])
@@ -84,26 +95,14 @@
     for load in loads:
         load.start()
 
-    y_order = sorted(range(n_y), key=lambda d: -min(d, n_y - d))
-
     def exchange(src, dst, phase):
-        def send(away_y, away_z):
-            target = lax.rem(my_y + away_y, n_y) * n_z + lax.rem(my_z + away_z, n_z)
+        def send(target):
             pltpu.make_async_remote_copy(
                 src.at[target], dst.at[me], scan_send.at[phase], scan_recv.at[phase],
                 device_id={"ctx": target, "head": mine}, device_id_type=MESH,
             ).start()
 
-        def step(i, carry):
-            away_z = n_z // 2 + ((i + 1) // 2) * (1 - 2 * lax.rem(i, 2))
-            for away_y in y_order:
-                send(away_y, away_z)
-            return carry
-
-        lax.fori_loop(0, n_z - 1, step, 0)
-        for away_y in y_order:
-            if away_y:
-                send(away_y, 0)
+        farthest_first(send)
         dst[pl.ds(me, 1)] = src[pl.ds(me, 1)]
 
     def arrived(dst, phase):
@@ -155,7 +154,7 @@
         jnp.int32, (HALF, HALF), 1
     )
     no_halo = jnp.where(me == 0, -1e30, 0.0).astype(F32)
-    scaled_t[...] = (gain[...].astype(F32) * cot[...].astype(F32)).T
+    scaled_t[...] = (gain[...].astype(F32).reshape(1, 256) * cot[...].astype(F32)).T
 
     def near(b, h, own, halo):
         prev_part = halo[:, cols[h]] if b == 0 else own[half[0], cols[h]]
@@ -277,16 +276,12 @@
         copy.start()
     for h in range(2):
         backward(1, h)
-    store_dq = pltpu.make_async_copy(dq, dq_hbm, out_sem.at[0])
-    store_dq.start()
 
     arrived(got_b, 2)
     running(got_b, back_b, range(n_ctx - 1, -1, -1))
     exchange(back_b, post, 3)
 
-    out[...] = ((local[...] * recip).T * gain[...].astype(F32)).astype(BF16)
-    store_out = pltpu.make_async_copy(out, out_hbm, out_sem.at[1])
-    store_out.start()
+    out[...] = ((local[...] * recip).T * gain[...].astype(F32).reshape(1, 256)).astype(BF16)
     for copy in halo_back:
         copy.wait()
     dk_acc[half[1], :] += dk_take[...].astype(F32)
@@ -294,22 +289,29 @@
 
     arrived(post, 3)
     collect(post, flat)
-    suffix = flat[...].astype(BF16)
-    for h in range(2):
-        dk[:, cols[h]] = (dk_acc[:, cols[h]] + nn(v[:, cols[h]], suffix[cols[h], :])).astype(BF16)
-    store_dk = pltpu.make_async_copy(dk, dk_hbm, out_sem.at[2])
-    store_dk.start()
-    for h in range(2):
-        dv[:, cols[h]] = (dv_acc[:, cols[h]] + nt(k[:, cols[h]], suffix[cols[h], :])).astype(BF16)
-    store_dv = pltpu.make_async_copy(dv, dv_hbm, out_sem.at[3])
-    store_dv.start()
-
+    suffix[...] = flat[...].astype(BF16)
     for phase, src in enumerate((scat_f, back_f, scat_b, back_b)):
         left(src, phase)
     sent = stat_all.at[pl.ds(0, n_head - 1)]
     pltpu.make_async_copy(sent, sent, stat_send).wait()
-    for copy in (store_dq, store_out, store_dk, store_dv):
-        copy.wait()
+
+
+def finish(out, dq, dk_acc, dv_acc, suffix, k, v, out_hbm, dq_hbm, dk_hbm, dv_hbm, dk, dv, sem):
+    stores = [
+        pltpu.make_async_copy(src, dst, sem.at[i])
+        for i, (src, dst) in enumerate(((out, out_hbm), (dq, dq_hbm), (dk, dk_hbm), (dv, dv_hbm)))
+    ]
+    stores[0].start()
+    stores[1].start()
+    cols = [slice(h * HEAD_DIM, (h + 1) * HEAD_DIM) for h in range(2)]
+    for c in cols:
+        dk[:, c] = (dk_acc[:, c] + nn(v[:, c], suffix[c, :])).astype(BF16)
+    stores[2].start()
+    for c in cols:
+        dv[:, c] = (dv_acc[:, c] + nt(k[:, c], suffix[c, :])).astype(BF16)
+    stores[3].start()
+    for store in stores:
+        store.wait()
 
 
 def on_device(n_ctx, n_z, n_head, queries, keys, values, gain, cotangent):
@@ -321,13 +323,20 @@
     piece = pltpu.VMEM(pieces, BF16)
     square = (2, 2, HALF, HALF)
     turned = (width, tokens)
-    return pl.pallas_call(
+    operands = (queries, keys, values, gain, cotangent)
+    summed = jax.ShapeDtypeStruct((tokens, width), F32)
+    vmem = pl.BlockSpec(memory_space=pltpu.VMEM)
+    anywhere = pl.BlockSpec(memory_space=pl.ANY)
+    results = pl.pallas_call(
         functools.partial(kernel, n_ctx, n_z, n_head),
-        out_shape=[block] * 4,
-        in_specs=[pl.BlockSpec(memory_space=pl.ANY)] * 5,
-        out_specs=[pl.BlockSpec(memory_space=pl.ANY)] * 4,
+        out_shape=[
+            block, block, summed, summed, jax.ShapeDtypeStruct((width, HEAD_DIM), BF16), block,
+            block,
+        ],
+        in_specs=[anywhere] * 5,
+        out_specs=[vmem] * 7,
         scratch_shapes=[
-            wide, wide, wide, pltpu.VMEM((1, width), BF16), wide,
+            wide, pltpu.VMEM((width,), BF16), wide,
             halo, halo, halo, halo, halo, halo,
             piece, piece, piece, piece, piece, piece, piece, piece,
             pltpu.VMEM((256, HEAD_DIM), F32),
@@ -335,9 +344,7 @@
             pltpu.VMEM(square, F32), pltpu.VMEM(square, BF16), pltpu.VMEM(square, BF16),
             pltpu.VMEM(turned, F32), pltpu.VMEM(turned, F32),
             pltpu.VMEM(turned, BF16), pltpu.VMEM(turned, BF16),
-            pltpu.VMEM((tokens, width), F32), pltpu.VMEM((tokens, width), F32),
-            wide, wide, wide, wide,
-            pltpu.SemaphoreType.DMA((5,)), pltpu.SemaphoreType.DMA((4,)),
+            pltpu.SemaphoreType.DMA((5,)),
             pltpu.SemaphoreType.DMA((4,)), pltpu.SemaphoreType.DMA((4,)),
             pltpu.SemaphoreType.DMA((4,)), pltpu.SemaphoreType.DMA((4,)),
             pltpu.SemaphoreType.DMA, pltpu.SemaphoreType.DMA,
@@ -345,7 +352,15 @@
         compiler_params=pltpu.CompilerParams(
             collective_id=0, has_side_effects=True, vmem_limit_bytes=48 << 20
         ),
-    )(queries, keys, values, gain.reshape(1, width), cotangent)
+    )(*[pltpu.with_memory_space_constraint(x, pltpu.HBM) for x in operands])
+    return pl.pallas_call(
+        finish,
+        out_shape=[block] * 4,
+        in_specs=[vmem] * 7,
+        out_specs=[anywhere] * 4,
+        scratch_shapes=[wide, wide, pltpu.SemaphoreType.DMA((4,))],
+        compiler_params=pltpu.CompilerParams(vmem_limit_bytes=32 << 20),
+    )(*[pltpu.with_memory_space_constraint(x, pltpu.VMEM) for x in results])
 
 
 def solution(mesh):

time: 67.4 us -> 59.8 us (0.89)
  local copies, waits for them, and re-layouts: 7.27 us -> 0 us
    unnamed x12 -> x0, local copies, waits for them, and re-layouts: 6.61 us -> none
    pallas_call x1, Pallas kernels: 59.2 us -> 57.9 us  [on_device(): pl.pallas_call(functools.partial(kernel, n_ctx, n_z, n_head), out_shape=[...]
    pallas_call x0 -> x1, Pallas kernels: none -> 1.04 us  [on_device(): pl.pallas_call(finish, out_shape=[block] * 4, in_specs=[vmem] * 7, out_sp...]
where the time goes in v2:
time: 59.8 us; the launch traced here: 59.6 us
  Pallas kernels  59 us (99%)
  between operations  0.64 us (1%)
    pallas_call x1, Pallas kernels, on_device(): pl.pallas_call(functools.partial(kernel, n_ctx, n_z, n_head), out_shape=[...  57.9 us

profile of v2, /device:TPU:1, one launch (start us, length us, event | category | flops | bytes accessed | tf_op | source)
XLA Modules:
  0.0 59.6 jit_solution(14189830218995909182)
XLA Ops:
  0.6 57.9 %shard_map.84 = (bf16[512,256]{1,0:T(8,128)(2,1)S(1)}, bf16[512,256]{1,0:T(8,128)(2,1)S(1)}, f32[512,256]{1,0:T(8,128)S(1)}, f32[512,256]{1,0:T(8,128)S(1)}, bf1...) custom-call(bf16[512,256]{1,0:T(8,128)(2,1)} %q_hbm.1, ...), custom_call_target="tpu_custom_call" | custom-call | tf_op jit(solution)/shard_map/pallas_call | solution.py:330
  58.6 1.0 %shard_map.85 = (bf16[512,256]{1,0:T(8,128)(2,1)}, bf16[512,256]{1,0:T(8,128)(2,1)}, bf16[512,256]{1,0:T(8,128)(2,1)}, bf16[512,256]{1,0:T(8,128)(2,1)}) custom-call(bf16[512,256]{1,0:T(8,128)(2,1)S(1)} %get-tuple-element.11.out, bf16[512,256]{1,0:T(8,128)(2,1)S(1)} %get-tuple-element.12.dq, f32[512,256]{1,0:T(8,128)S(1)} %get-tuple-element.13.dk_acc, ...), custom_call_target="tpu_custom_call" | custom-call | tf_op jit(solution)/shard_map/pallas_call | solution.py:356

commit v3 on v2

--- a/solution.py
+++ b/solution.py
@@ -41,10 +41,10 @@
     out, dq, dk_acc, dv_acc, suffix, k, v,
     q, gain, cot,
     k_halo, v_halo, dk_give, dv_give, dk_take, dv_take,
-    scat_f, got_f, back_f, pre, scat_b, got_b, back_b, post, flat,
+    scat_f, mid, got_f, back_f, pre, scat_b, got_b, back_b, post, flat,
     stat_mine, stat_all,
     probs, w_own, w_prev, local, scaled_t, grad_t, gradu_t,
-    in_sem, scan_send, scan_recv, halo_send, halo_recv, stat_send, stat_recv,
+    in_sem, leg_send, leg_recv, known, scan_send, scan_recv, halo_send, halo_recv, stat_send, stat_recv,
 ):
     me = lax.axis_index("ctx")
     mine = lax.axis_index("head")
@@ -60,6 +60,11 @@
 
     barrier = pltpu.get_barrier_semaphore()
 
+    reach = max(1, n_z // 4)
+
+    def at_z(step):
+        return my_y * n_z + lax.rem(my_z + step, n_z)
+
     y_order = sorted(range(n_y), key=lambda d: -min(d, n_y - d))
 
     def farthest_first(visit):
@@ -82,9 +87,15 @@
             barrier, inc=1, device_id={"ctx": target, "head": head}, device_id_type=MESH
         )
 
-    farthest_first(lambda target: greet(target, mine))
+    for step in range(1, n_y):
+        greet(lax.rem(my_y + step, n_y) * n_z + my_z, mine)
+    for step in range(reach, 0, -1):
+        greet(at_z(step), mine)
+        greet(at_z(n_z - step), mine)
     for step in range(1, n_head):
         greet(me, lax.rem(mine + step, n_head))
+    greet(following, mine)
+    greet(before, mine)
 
     loads = [
         pltpu.make_async_copy(src, dst, in_sem.at[i])
@@ -121,7 +132,7 @@
         total = jnp.zeros((rows, HEAD_DIM), F32)
         for i in order:
             dst[i] = total.astype(BF16)
-            total = total + src[i].astype(F32)
+            total = total + src(i).astype(F32)
 
     def collect(src, dst):
         for i in range(n_ctx):
@@ -134,18 +145,18 @@
     loads[1].wait()
     for h in range(2):
         scatter(tn(v[:, cols[h]], k[:, cols[h]]), h, scat_f)
-    pl.semaphore_wait(barrier, n_ctx - 1 + n_head - 1)
-    exchange(scat_f, got_f, 0)
-    halo_out = [
+    pl.semaphore_wait(barrier, n_y - 1 + 2 * reach + n_head - 1 + 2)
+    for step in range(1, n_y):
+        other = lax.rem(my_y + step, n_y)
         pltpu.make_async_remote_copy(
-            src.at[pl.ds(HALF, HALF)], dst, halo_send.at[i], halo_recv.at[i],
-            device_id={"ctx": following, "head": mine}, device_id_type=MESH,
-        )
-        for i, (src, dst) in enumerate(((k, k_halo), (v, v_halo)))
-    ]
-    for copy in halo_out:
-        copy.start()
-
+            scat_f.at[pl.ds(other * n_z, n_z)], mid.at[my_y], leg_send.at[0], leg_recv.at[0],
+            device_id={"ctx": other * n_z + my_z, "head": mine}, device_id_type=MESH,
+        ).start()
+    for step in (reach, n_z - reach):
+        pl.semaphore_signal(
+            known, inc=1, device_id={"ctx": at_z(step), "head": mine}, device_id_type=MESH
+        )
+    mid[pl.ds(my_y, 1)] = scat_f[pl.ds(my_y * n_z, n_z)][None]
     for load in loads[2:]:
         load.wait()
     position = me * tokens + lax.broadcasted_iota(jnp.int32, (1, tokens), 1)
@@ -183,15 +194,36 @@
 
     for h in range(2):
         forward(1, h)
+    whole = mid.at[pl.ds(0, n_y - 1)]
+    pltpu.make_async_copy(whole, whole, leg_recv.at[0]).wait()
+    pl.semaphore_wait(known, 2)
+    for step in sorted(range(1, n_z), key=lambda d: -min(d, n_z - d)):
+        other = lax.rem(my_z + step, n_z)
+        pltpu.make_async_remote_copy(
+            mid.at[:, other], got_f.at[my_z], leg_send.at[1], leg_recv.at[1],
+            device_id={"ctx": at_z(step), "head": mine}, device_id_type=MESH,
+        ).start()
+    got_f[pl.ds(my_z, 1)] = mid[:, pl.ds(my_z, 1)].reshape(1, n_y, rows, HEAD_DIM)
+    halo_out = [
+        pltpu.make_async_remote_copy(
+            src.at[pl.ds(HALF, HALF)], dst, halo_send.at[i], halo_recv.at[i],
+            device_id={"ctx": following, "head": mine}, device_id_type=MESH,
+        )
+        for i, (src, dst) in enumerate(((k, k_halo), (v, v_halo)))
+    ]
+    for copy in halo_out:
+        copy.start()
+
     for copy in halo_out:
         copy.wait()
     for h in range(2):
         forward(0, h)
 
-    arrived(got_f, 0)
-    running(got_f, back_f, range(n_ctx))
-    exchange(back_f, pre, 1)
-    arrived(pre, 1)
+    part = got_f.at[pl.ds(0, n_z - 1)]
+    pltpu.make_async_copy(part, part, leg_recv.at[1]).wait()
+    running(lambda i: got_f[i % n_z, i // n_z], back_f, range(n_ctx))
+    exchange(back_f, pre, 0)
+    arrived(pre, 0)
     collect(pre, flat)
     prefix = flat[...].astype(BF16)
 
@@ -230,7 +262,7 @@
         grad_u = (full * coef).astype(BF16)
         gradu_t[cols[h], :] = grad_u
         scatter(nn(grad_u, q[:, cols[h]]), h, scat_b)
-    exchange(scat_b, got_b, 2)
+    exchange(scat_b, got_b, 1)
 
     dk_acc[...] = jnp.zeros_like(dk_acc)
     dv_acc[...] = jnp.zeros_like(dv_acc)
@@ -277,9 +309,9 @@
     for h in range(2):
         backward(1, h)
 
-    arrived(got_b, 2)
-    running(got_b, back_b, range(n_ctx - 1, -1, -1))
-    exchange(back_b, post, 3)
+    arrived(got_b, 1)
+    running(lambda i: got_b[i], back_b, range(n_ctx - 1, -1, -1))
+    exchange(back_b, post, 2)
 
     out[...] = ((local[...] * recip).T * gain[...].astype(F32).reshape(1, 256)).astype(BF16)
     for copy in halo_back:
@@ -287,11 +319,13 @@
     dk_acc[half[1], :] += dk_take[...].astype(F32)
     dv_acc[half[1], :] += dv_take[...].astype(F32)
 
-    arrived(post, 3)
+    arrived(post, 2)
     collect(post, flat)
     suffix[...] = flat[...].astype(BF16)
-    for phase, src in enumerate((scat_f, back_f, scat_b, back_b)):
+    for phase, src in enumerate((back_f, scat_b, back_b)):
         left(src, phase)
+    pltpu.make_async_copy(whole, whole, leg_send.at[0]).wait()
+    pltpu.make_async_copy(part, part, leg_send.at[1]).wait()
     sent = stat_all.at[pl.ds(0, n_head - 1)]
     pltpu.make_async_copy(sent, sent, stat_send).wait()
 
@@ -316,6 +350,7 @@
 
 def on_device(n_ctx, n_z, n_head, queries, keys, values, gain, cotangent):
     tokens, width = queries.shape
+    n_y = n_ctx // n_z
     pieces = (n_ctx, 256 // n_ctx, HEAD_DIM)
     block = jax.ShapeDtypeStruct((tokens, width), BF16)
     wide = pltpu.VMEM((tokens, width), BF16)
@@ -338,14 +373,17 @@
         scratch_shapes=[
             wide, pltpu.VMEM((width,), BF16), wide,
             halo, halo, halo, halo, halo, halo,
-            piece, piece, piece, piece, piece, piece, piece, piece,
+            piece, pltpu.VMEM((n_y, n_z, *pieces[1:]), BF16),
+            pltpu.VMEM((n_z, n_y, *pieces[1:]), BF16), piece, piece, piece, piece, piece, piece,
             pltpu.VMEM((256, HEAD_DIM), F32),
             pltpu.VMEM((2, tokens), F32), pltpu.VMEM((n_head, 2, tokens), F32),
             pltpu.VMEM(square, F32), pltpu.VMEM(square, BF16), pltpu.VMEM(square, BF16),
             pltpu.VMEM(turned, F32), pltpu.VMEM(turned, F32),
             pltpu.VMEM(turned, BF16), pltpu.VMEM(turned, BF16),
             pltpu.SemaphoreType.DMA((5,)),
-            pltpu.SemaphoreType.DMA((4,)), pltpu.SemaphoreType.DMA((4,)),
+            pltpu.SemaphoreType.DMA((2,)), pltpu.SemaphoreType.DMA((2,)),
+            pltpu.SemaphoreType.REGULAR,
+            pltpu.SemaphoreType.DMA((3,)), pltpu.SemaphoreType.DMA((3,)),
             pltpu.SemaphoreType.DMA((4,)), pltpu.SemaphoreType.DMA((4,)),
             pltpu.SemaphoreType.DMA, pltpu.SemaphoreType.DMA,
         ],

time: 59.8 us -> 60.1 us (level)
  no operation moved by 1% of the time
where the time goes in v3:
time: 60.1 us; the launch traced here: 60 us
  Pallas kernels  59.3 us (99%)
  between operations  0.64 us (1%)
    pallas_call x1, Pallas kernels, on_device(): pl.pallas_call(functools.partial(kernel, n_ctx, n_z, n_head), out_shape=[...  58.3 us

profile of v3, /device:TPU:1, one launch (start us, length us, event | category | flops | bytes accessed | tf_op | source)
XLA Modules:
  0.0 60.0 jit_solution(11269190685757852046)
XLA Ops:
  0.6 58.3 %shard_map.84 = (bf16[512,256]{1,0:T(8,128)(2,1)S(1)}, bf16[512,256]{1,0:T(8,128)(2,1)S(1)}, f32[512,256]{1,0:T(8,128)S(1)}, f32[512,256]{1,0:T(8,128)S(1)}, bf1...) custom-call(bf16[512,256]{1,0:T(8,128)(2,1)} %q_hbm.1, ...), custom_call_target="tpu_custom_call" | custom-call | tf_op jit(solution)/shard_map/pallas_call | solution.py:365
  58.9 1.0 %shard_map.85 = (bf16[512,256]{1,0:T(8,128)(2,1)}, bf16[512,256]{1,0:T(8,128)(2,1)}, bf16[512,256]{1,0:T(8,128)(2,1)}, bf16[512,256]{1,0:T(8,128)(2,1)}) custom-call(bf16[512,256]{1,0:T(8,128)(2,1)S(1)} %get-tuple-element.11.out, bf16[512,256]{1,0:T(8,128)(2,1)S(1)} %get-tuple-element.12.dq, f32[512,256]{1,0:T(8,128)S(1)} %get-tuple-element.13.dk_acc, ...), custom_call_target="tpu_custom_call" | custom-call | tf_op jit(solution)/shard_map/pallas_call | solution.py:394

commit v4 on v3

--- a/solution.py
+++ b/solution.py
@@ -60,7 +60,10 @@
 
     barrier = pltpu.get_barrier_semaphore()
 
-    reach = max(1, n_z // 4)
+    reach = max(1, n_z // 8)
+    relays = []
+    while reach << len(relays) < n_z // 2:
+        relays.append(reach << len(relays))
 
     def at_z(step):
         return my_y * n_z + lax.rem(my_z + step, n_z)
@@ -152,11 +155,34 @@
             scat_f.at[pl.ds(other * n_z, n_z)], mid.at[my_y], leg_send.at[0], leg_recv.at[0],
             device_id={"ctx": other * n_z + my_z, "head": mine}, device_id_type=MESH,
         ).start()
-    for step in (reach, n_z - reach):
-        pl.semaphore_signal(
-            known, inc=1, device_id={"ctx": at_z(step), "head": mine}, device_id_type=MESH
+    def halo_copy(i, src, dst, first, count):
+        return pltpu.make_async_remote_copy(
+            src.at[pl.ds(HALF + first, count)], dst.at[pl.ds(first, count)],
+            halo_send.at[i], halo_recv.at[i],
+            device_id={"ctx": following, "head": mine}, device_id_type=MESH,
         )
+
+    halo_out = [
+        halo_copy(0, k, k_halo, 0, HALF),
+        halo_copy(1, v, v_halo, 0, HALF // 2),
+        halo_copy(4, v, v_halo, HALF // 2, HALF // 2),
+    ]
+
     mid[pl.ds(my_y, 1)] = scat_f[pl.ds(my_y * n_z, n_z)][None]
+
+    def relay(i):
+        for step in (relays[i], n_z - relays[i]):
+            pl.semaphore_signal(
+                known.at[i], inc=1, device_id={"ctx": at_z(step), "head": mine},
+                device_id_type=MESH,
+            )
+
+    for i in range(len(relays)):
+        if i:
+            pl.semaphore_wait(known.at[i - 1], 2)
+        relay(i)
+        if i == 0:
+            halo_out[0].start()
     for load in loads[2:]:
         load.wait()
     position = me * tokens + lax.broadcasted_iota(jnp.int32, (1, tokens), 1)
@@ -196,33 +222,26 @@
         forward(1, h)
     whole = mid.at[pl.ds(0, n_y - 1)]
     pltpu.make_async_copy(whole, whole, leg_recv.at[0]).wait()
-    pl.semaphore_wait(known, 2)
+    if relays:
+        pl.semaphore_wait(known.at[len(relays) - 1], 2)
     for step in sorted(range(1, n_z), key=lambda d: -min(d, n_z - d)):
         other = lax.rem(my_z + step, n_z)
         pltpu.make_async_remote_copy(
             mid.at[:, other], got_f.at[my_z], leg_send.at[1], leg_recv.at[1],
             device_id={"ctx": at_z(step), "head": mine}, device_id_type=MESH,
         ).start()
+    halo_out[1].start()
     got_f[pl.ds(my_z, 1)] = mid[:, pl.ds(my_z, 1)].reshape(1, n_y, rows, HEAD_DIM)
-    halo_out = [
-        pltpu.make_async_remote_copy(
-            src.at[pl.ds(HALF, HALF)], dst, halo_send.at[i], halo_recv.at[i],
-            device_id={"ctx": following, "head": mine}, device_id_type=MESH,
-        )
-        for i, (src, dst) in enumerate(((k, k_halo), (v, v_halo)))
-    ]
-    for copy in halo_out:
-        copy.start()
-
-    for copy in halo_out:
-        copy.wait()
-    for h in range(2):
-        forward(0, h)
-
     part = got_f.at[pl.ds(0, n_z - 1)]
     pltpu.make_async_copy(part, part, leg_recv.at[1]).wait()
     running(lambda i: got_f[i % n_z, i // n_z], back_f, range(n_ctx))
     exchange(back_f, pre, 0)
+    halo_out[1].wait()
+    halo_out[2].start()
+    halo_out[0].wait()
+    halo_out[2].wait()
+    for h in range(2):
+        forward(0, h)
     arrived(pre, 0)
     collect(pre, flat)
     prefix = flat[...].astype(BF16)
@@ -382,9 +401,9 @@
             pltpu.VMEM(turned, BF16), pltpu.VMEM(turned, BF16),
             pltpu.SemaphoreType.DMA((5,)),
             pltpu.SemaphoreType.DMA((2,)), pltpu.SemaphoreType.DMA((2,)),
-            pltpu.SemaphoreType.REGULAR,
+            pltpu.SemaphoreType.REGULAR((4,)),
             pltpu.SemaphoreType.DMA((3,)), pltpu.SemaphoreType.DMA((3,)),
-            pltpu.SemaphoreType.DMA((4,)), pltpu.SemaphoreType.DMA((4,)),
+            pltpu.SemaphoreType.DMA((5,)), pltpu.SemaphoreType.DMA((5,)),
             pltpu.SemaphoreType.DMA, pltpu.SemaphoreType.DMA,
         ],
         compiler_params=pltpu.CompilerParams(

time: 60.1 us -> 56.6 us (0.942)
  Pallas kernels: 59.3 us -> 55.6 us
    pallas_call x1, Pallas kernels: 58.3 us -> 54.6 us  [on_device(): pl.pallas_call(functools.partial(kernel, n_ctx, n_z, n_head), out_shape=[...]
where the time goes in v4:
time: 56.6 us; the launch traced here: 56.3 us
  Pallas kernels  55.6 us (98%)
  between operations  0.64 us (1%)
    pallas_call x1, Pallas kernels, on_device(): pl.pallas_call(functools.partial(kernel, n_ctx, n_z, n_head), out_shape=[...  54.6 us

profile of v4, /device:TPU:1, one launch (start us, length us, event | category | flops | bytes accessed | tf_op | source)
XLA Modules:
  0.0 56.3 jit_solution(9568004908154076218)
XLA Ops:
  0.6 54.6 %shard_map.84 = (bf16[512,256]{1,0:T(8,128)(2,1)S(1)}, bf16[512,256]{1,0:T(8,128)(2,1)S(1)}, f32[512,256]{1,0:T(8,128)S(1)}, f32[512,256]{1,0:T(8,128)S(1)}, bf1...) custom-call(bf16[512,256]{1,0:T(8,128)(2,1)} %q_hbm.1, ...), custom_call_target="tpu_custom_call" | custom-call | tf_op jit(solution)/shard_map/pallas_call | solution.py:384
  55.2 1.0 %shard_map.85 = (bf16[512,256]{1,0:T(8,128)(2,1)}, bf16[512,256]{1,0:T(8,128)(2,1)}, bf16[512,256]{1,0:T(8,128)(2,1)}, bf16[512,256]{1,0:T(8,128)(2,1)}) custom-call(bf16[512,256]{1,0:T(8,128)(2,1)S(1)} %get-tuple-element.11.out, bf16[512,256]{1,0:T(8,128)(2,1)S(1)} %get-tuple-element.12.dq, f32[512,256]{1,0:T(8,128)S(1)} %get-tuple-element.13.dk_acc, ...), custom_call_target="tpu_custom_call" | custom-call | tf_op jit(solution)/shard_map/pallas_call | solution.py:413

commit v5 on v4

--- a/solution.py
+++ b/solution.py
@@ -323,14 +323,14 @@
         )
         for i, (src, dst) in enumerate(((dk_give, dk_take), (dv_give, dv_take)))
     ]
-    for copy in halo_back:
-        copy.start()
+    halo_back[0].start()
     for h in range(2):
         backward(1, h)
 
     arrived(got_b, 1)
     running(lambda i: got_b[i], back_b, range(n_ctx - 1, -1, -1))
     exchange(back_b, post, 2)
+    halo_back[1].start()
 
     out[...] = ((local[...] * recip).T * gain[...].astype(F32).reshape(1, 256)).astype(BF16)
     for copy in halo_back:
@@ -350,19 +350,27 @@
 
 
 def finish(out, dq, dk_acc, dv_acc, suffix, k, v, out_hbm, dq_hbm, dk_hbm, dv_hbm, dk, dv, sem):
+    cols = [slice(h * HEAD_DIM, (h + 1) * HEAD_DIM) for h in range(2)]
     stores = [
-        pltpu.make_async_copy(src, dst, sem.at[i])
-        for i, (src, dst) in enumerate(((out, out_hbm), (dq, dq_hbm), (dk, dk_hbm), (dv, dv_hbm)))
+        pltpu.make_async_copy(out, out_hbm, sem.at[0]), pltpu.make_async_copy(dq, dq_hbm, sem.at[1])
     ]
-    stores[0].start()
-    stores[1].start()
-    cols = [slice(h * HEAD_DIM, (h + 1) * HEAD_DIM) for h in range(2)]
-    for c in cols:
-        dk[:, c] = (dk_acc[:, c] + nn(v[:, c], suffix[c, :])).astype(BF16)
-    stores[2].start()
-    for c in cols:
-        dv[:, c] = (dv_acc[:, c] + nt(k[:, c], suffix[c, :])).astype(BF16)
-    stores[3].start()
+    for store in stores:
+        store.start()
+
+    def hand_on(src, dst, first, i):
+        part = pl.ds(first, HALF)
+        store = pltpu.make_async_copy(src.at[part], dst.at[part], sem.at[i])
+        store.start()
+        stores.append(store)
+
+    for b in range(2):
+        half = slice(b * HALF, (b + 1) * HALF)
+        for c in cols:
+            dk[half, c] = (dk_acc[half, c] + nn(v[half, c], suffix[c, :])).astype(BF16)
+        hand_on(dk, dk_hbm, b * HALF, 2 + 2 * b)
+        for c in cols:
+            dv[half, c] = (dv_acc[half, c] + nt(k[half, c], suffix[c, :])).astype(BF16)
+        hand_on(dv, dv_hbm, b * HALF, 3 + 2 * b)
     for store in stores:
         store.wait()
 
@@ -415,7 +423,7 @@
         out_shape=[block] * 4,
         in_specs=[vmem] * 7,
         out_specs=[anywhere] * 4,
-        scratch_shapes=[wide, wide, pltpu.SemaphoreType.DMA((4,))],
+        scratch_shapes=[wide, wide, pltpu.SemaphoreType.DMA((6,))],
         compiler_params=pltpu.CompilerParams(vmem_limit_bytes=32 << 20),
     )(*[pltpu.with_memory_space_constraint(x, pltpu.VMEM) for x in results])
 

time: 56.6 us -> 56.6 us (level)
  no operation moved by 1% of the time
where the time goes in v5:
time: 56.6 us; the launch traced here: 56.2 us
  Pallas kernels  55.6 us (98%)
  between operations  0.64 us (1%)
    pallas_call x1, Pallas kernels, on_device(): pl.pallas_call(functools.partial(kernel, n_ctx, n_z, n_head), out_shape=[...  54.6 us

profile of v5, /device:TPU:1, one launch (start us, length us, event | category | flops | bytes accessed | tf_op | source)
XLA Modules:
  0.0 56.2 jit_solution(4734152783021692545)
XLA Ops:
  0.6 54.6 %shard_map.84 = (bf16[512,256]{1,0:T(8,128)(2,1)S(1)}, bf16[512,256]{1,0:T(8,128)(2,1)S(1)}, f32[512,256]{1,0:T(8,128)S(1)}, f32[512,256]{1,0:T(8,128)S(1)}, bf1...) custom-call(bf16[512,256]{1,0:T(8,128)(2,1)} %q_hbm.1, ...), custom_call_target="tpu_custom_call" | custom-call | tf_op jit(solution)/shard_map/pallas_call | solution.py:392
  55.2 1.0 %shard_map.85 = (bf16[512,256]{1,0:T(8,128)(2,1)}, bf16[512,256]{1,0:T(8,128)(2,1)}, bf16[512,256]{1,0:T(8,128)(2,1)}, bf16[512,256]{1,0:T(8,128)(2,1)}) custom-call(bf16[512,256]{1,0:T(8,128)(2,1)S(1)} %get-tuple-element.11.out, bf16[512,256]{1,0:T(8,128)(2,1)S(1)} %get-tuple-element.12.dq, f32[512,256]{1,0:T(8,128)S(1)} %get-tuple-element.13.dk_acc, ...), custom_call_target="tpu_custom_call" | custom-call | tf_op jit(solution)/shard_map/pallas_call | solution.py:421

commit v6 on v5

--- a/solution.py
+++ b/solution.py
@@ -260,7 +260,7 @@
             stat_mine, stat_all.at[mine], stat_send, stat_recv,
             device_id={"ctx": me, "head": lax.rem(mine + step, n_head)}, device_id_type=MESH,
         )
-        for step in range(n_head - 1, 0, -1)
+        for step in sorted(range(1, n_head), key=lambda d: -min(d, n_head - d))
     ]
     for copy in shares:
         copy.start()

time: 56.6 us -> 56.7 us (level)
  no operation moved by 1% of the time
where the time goes in v6:
time: 56.7 us; the launch traced here: 56.5 us
  Pallas kernels  55.9 us (99%)
  between operations  0.64 us (1%)
    pallas_call x1, Pallas kernels, on_device(): pl.pallas_call(functools.partial(kernel, n_ctx, n_z, n_head), out_shape=[...  54.9 us

profile of v6, /device:TPU:1, one launch (start us, length us, event | category | flops | bytes accessed | tf_op | source)
XLA Modules:
  0.0 56.5 jit_solution(11977555445736065243)
XLA Ops:
  0.6 54.9 %shard_map.84 = (bf16[512,256]{1,0:T(8,128)(2,1)S(1)}, bf16[512,256]{1,0:T(8,128)(2,1)S(1)}, f32[512,256]{1,0:T(8,128)S(1)}, f32[512,256]{1,0:T(8,128)S(1)}, bf1...) custom-call(bf16[512,256]{1,0:T(8,128)(2,1)} %q_hbm.1, ...), custom_call_target="tpu_custom_call" | custom-call | tf_op jit(solution)/shard_map/pallas_call | solution.py:392
  55.5 1.0 %shard_map.85 = (bf16[512,256]{1,0:T(8,128)(2,1)}, bf16[512,256]{1,0:T(8,128)(2,1)}, bf16[512,256]{1,0:T(8,128)(2,1)}, bf16[512,256]{1,0:T(8,128)(2,1)}) custom-call(bf16[512,256]{1,0:T(8,128)(2,1)S(1)} %get-tuple-element.11.out, bf16[512,256]{1,0:T(8,128)(2,1)S(1)} %get-tuple-element.12.dq, f32[512,256]{1,0:T(8,128)S(1)} %get-tuple-element.13.dk_acc, ...), custom_call_target="tpu_custom_call" | custom-call | tf_op jit(solution)/shard_map/pallas_call | solution.py:421
